TPU v7x, 128 devices: a whole 4x4x4 slice. The times are simulated.
128 devices in a mesh: visit: 4 (over x), patch: 32 (over z, y, core).
Axes of the slice: x: 4, y: 4, z: 4, core: 2. Of those that a mesh axis runs over, the one named last changes fastest.
Arguments:
- image: float32 [4096, 128, 128], P(('visit', 'patch')), may hold values from -6 to 6
- variance: float32 [4096, 128, 128], P(('visit', 'patch')), may hold values from 0.25 to 4
- intersections: int32 [4096, 2], P(('visit', 'patch')), may hold values from 0 to 31, all different within a row; in each aligned block of 32 rows (0 to 31, 32 to 63, ...) at most 3 rows name the same one
- boxes: int32 [4096, 2, 2], P(('visit', 'patch')), may hold values from -64 to 191
- shifts: float32 [4096, 2, 2], P(('visit', 'patch')), may hold values from 0 to 1
- basis_ids: int32 [4096, 3], P(('visit', 'patch')), may hold values from 0 to 7
- coefs: float32 [4096, 3], P(('visit', 'patch')), may hold values from 0.3 to 1.5
- taps: float32 [8, 2, 41], replicated, may hold values from -1 to 1
Outputs:
- coadd: float32 [8192, 256], P('patch')
- coadd_var: float32 [8192, 256], P('patch')
Inputs may be any that keep to these rules, and one draw needn't show every extreme that they name: `intersections`: the rows of one device name every patch at most 3 times; each tile names two different patches.
All inputs are finite; a program needn't handle non-finite values.
Results may differ from a plain program's by a relative error of at most 0.0003.
Values sent between devices are 32-bit elements; how exact they have to be, the bound alone decides.
No kernel may reach another device: no remote copies, remote signals or barrier semaphores. Data moves between devices by JAX's collectives and lax.ppermute only.
A program may use at most 128 MiB of HBM per device.

v0:
```python
import jax
import jax.numpy as jnp
from jax import lax
from jax.sharding import PartitionSpec as P

PATCH = 256
HI = lax.Precision.HIGHEST
group_width = 8


def band_table(side, ntaps):
    offs = jnp.arange(side)[:, None] - jnp.arange(side)[None, :] + (ntaps - 1) // 2
    return (offs[:, :, None] == jnp.arange(ntaps)[None, None, :]).astype(jnp.float32)


def convolve(images, row_taps, col_taps, weights_b):
    band = band_table(images.shape[-1], row_taps.shape[-1])
    row_mats = jnp.einsum("ikt,gbt->gbik", band, row_taps, precision=HI)
    col_mats = jnp.einsum("jlt,gbt->gbjl", band, col_taps, precision=HI)
    partial_rows = jnp.einsum("gbik,gkl->gbil", row_mats, images, precision=HI)
    scaled = partial_rows * weights_b[:, :, None, None]
    return jnp.einsum("gbil,gbjl->gij", scaled, col_mats, precision=HI)


def interpolation(offset, shift, count, side):
    place = (
        jnp.arange(count).astype(jnp.float32)[None, :, None]
        - offset[:, None, None]
        - shift[:, None, None]
        - jnp.arange(side).astype(jnp.float32)[None, None, :]
    )
    return jnp.maximum(0.0, 1.0 - jnp.abs(place))


def warp_group(planes, meta, patch_side):
    side = planes.shape[-1]
    rows_w = interpolation(meta[:, 1], meta[:, 3], patch_side, side)
    cols_w = interpolation(meta[:, 2], meta[:, 4], patch_side, side)
    left = jnp.einsum("gpi,gcij->gcpj", rows_w, planes, precision=HI)
    both = jnp.einsum("gcpj,gqj->gcpq", left, cols_w, precision=HI)
    weight = meta[:, 0]
    num = jnp.sum(weight[:, None, None] * both[:, 0], 0)
    vsum = jnp.sum((weight * weight)[:, None, None] * both[:, 1], 0)
    cover = jnp.sum(rows_w, 2)[:, :, None] * jnp.sum(cols_w, 2)[:, None, :]
    den = jnp.sum(weight[:, None, None] * cover, 0)
    return jnp.stack([num, den, vsum], 0)


def finish(num, den, vsum):
    safe = jnp.maximum(den, 1.0)
    return (num / safe, vsum / (safe * safe))


def basis_taps(ids, taps):
    select = (ids[..., None] == jnp.arange(taps.shape[0])[None, None, :]).astype(jnp.float32)
    row_t = jnp.einsum("gbn,nk->gbk", select, taps[:, 0], precision=HI)
    col_t = jnp.einsum("gbn,nk->gbk", select, taps[:, 1], precision=HI)
    return (row_t, col_t)


def shards(image, variance, intersections, boxes, shifts, basis_ids, coefs, taps):
    tiles = image.shape[0]
    side = image.shape[1]
    nterms = coefs.shape[1]
    peers = lax.axis_size("patch")
    capacity = max(2, 3 * tiles // peers)
    slots = peers * capacity
    dest = intersections.reshape(-1)
    count = dest.shape[0]
    order = jnp.arange(count)
    earlier = (dest[:, None] == dest[None, :]) & (order[None, :] < order[:, None])
    rank = jnp.sum(earlier.astype(jnp.int32), 1)
    slot_of = dest * capacity + rank
    match = slot_of[None, :] == jnp.arange(slots)[:, None]
    live = jnp.any(match, 1)
    item = jnp.sum(jnp.where(match, order[None, :], 0), 1)
    tile_of = item // 2
    livef = live.astype(jnp.float32)
    inverse_var = 1.0 / jnp.mean(variance, axis=(1, 2))
    box_flat = boxes.reshape(count, 2).astype(jnp.float32)[item]
    shift_flat = shifts.reshape(count, 2)[item]
    geometry = jnp.concatenate([(inverse_var[tile_of] * livef)[:, None], box_flat, shift_flat], 1)
    planes = jnp.stack([image, variance], 1)[tile_of] * livef[:, None, None, None]
    meta = jnp.concatenate([geometry, coefs[tile_of], basis_ids[tile_of].astype(jnp.float32)], 1)
    width = meta.shape[1]
    sent = planes.reshape(peers, capacity, 2, side, side)
    sent_meta = meta.reshape(peers, capacity, width)
    arrived, arrived_meta = (
        lax.all_to_all(sent, "patch", split_axis=0, concat_axis=0, tiled=True),
        lax.all_to_all(sent_meta, "patch", split_axis=0, concat_axis=0, tiled=True),
    )
    groups = slots // group_width
    arrived = arrived.reshape(groups, group_width, 2, side, side)
    arrived_meta = arrived_meta.reshape(groups, group_width, width)

    def accumulate(total, parts):
        block, block_meta = parts
        ids = block_meta[:, 5 + nterms : 5 + 2 * nterms].astype(jnp.int32)
        row_t, col_t = basis_taps(ids, taps)
        matched = convolve(block[:, 0], row_t, col_t, block_meta[:, 5 : 5 + nterms])
        block = jnp.stack([matched, block[:, 1]], 1)
        return (total + warp_group(block, block_meta, PATCH), None)

    start = jnp.zeros((3, PATCH, PATCH), jnp.float32)
    partial_value = lax.scan(accumulate, start, (arrived, arrived_meta))[0]
    total = lax.psum(partial_value, "visit")
    coadd, coadd_var = finish(total[0], total[1], total[2])
    return (coadd, coadd_var)


def solution(mesh):
    in_specs = (
        P(("visit", "patch"), None, None),
        P(("visit", "patch"), None, None),
        P(("visit", "patch"), None),
        P(("visit", "patch"), None, None),
        P(("visit", "patch"), None, None),
        P(("visit", "patch"), None),
        P(("visit", "patch"), None),
        P(),
    )
    out_specs = (P("patch", None), P("patch", None))
    return jax.shard_map(shards, mesh=mesh, in_specs=in_specs, out_specs=out_specs, check_vma=False)
```

profile of v0, /device:TPU:0, one launch (start us, length us, event | category | flops | bytes accessed | tf_op | source)
XLA Modules:
  0.0 473.0 jit_solution(7930241180158183529)
XLA Ops:
  8.5 1.9 reduce_sum.75
  16.5 8.4 %all-to-all-start = ((f32[32,3,11]{2,1,0:T(4,128)}), f32[32,3,11]{2,1,0:T(4,128)S(1)}, u32[]{:S(2)}, u32[]{:S(2)}) async-start(f32[32,3,11]{2,1,0:T(4,128)} %copy.90), calls=%async_computation | async-start | bytes 131072 | tf_op jit(solution)/shard_map/all_to_all | solution.py:90
  24.9 3.9 pad_maximum_fusion.1
  28.9 10.9 %gather_fusion.5 = f32[96,2,128,128]{3,2,1,0:T(8,128)} fusion(f32[32,2,128,128]{3,2,0,1:T(8,128)} %pad_maximum_fusion.1, s32[1024]{0:T(1024)S(1)} %get-tuple-element.97), kind=kCustom, calls=%fused_computation.5 | custom fusion | bytes 25166208 | tf_op jit(solution)/shard_map/gather | solution.py:83
  39.9 11.8 %broadcast_multiply_fusion = f32[32,3,2,128,128]{4,3,2,1,0:T(8,128)} fusion(f32[32,3,2,128,128]{4,3,2,1,0:T(8,128)} %bitcast.135, f32[32,3]{1,0:T(8,128)S(1)} %reshape.285), kind=kLoop, calls=%fused_computation.74 | loop fusion | flops 3145728 | bytes 25166208 | tf_op jit(solution)/shard_map/mul | solution.py:83
  51.6 7.6 %all-to-all-start.1 = ((f32[32,3,2,128,128]{4,3,2,1,0:T(8,128)}), f32[32,3,2,128,128]{4,3,2,1,0:T(8,128)}, u32[]{:S(2)}, u32[]{:S(2)}) async-start(f32[32,3,2,128,128]{4,3,2,1,0:T(8,128)} %broadcast_multiply_fusion), calls=%async_computation.1 | async-start | bytes 25165824 | tf_op jit(solution)/shard_map/all_to_all | solution.py:89
  59.4 160.7 %all-to-all-done.1 = f32[32,3,2,128,128]{4,3,2,1,0:T(8,128)} async-done(((f32[32,3,2,128,128]{4,3,2,1,0:T(8,128)}), f32[32,3,2,128,128]{4,3,2,1,0:T(8,128)}, u32[]{:S(2)}, u32[]{:S(2)}) %all-to-all-start.1) | async-done | bytes 12582944 | tf_op jit(solution)/shard_map/all_to_all | solution.py:89
  220.1 202.3 %while.11 = (s32[]{:T(128)}, f32[3,256,256]{2,1,0:T(8,128)S(1)}, f32[12,8,11]{2,1,0:T(8,128)S(1)}, f32[8,2,41]{2,0,1:T(8,128)S(1)}, f32[12,8,2,128,128]{4,3,2,1,0:T(8,128)}, /*index=5*/s32[]{:T(128)}, s32[]{:T(128)}) while((s32[]{:T(128)}, f32[3,256,256]{2,1,0:T(8,128)S(1)}, f32[12,8,11]{2,1,0:T(8,128)S(1)}, ...), condition=%wide.region_10.11_spmd.clone, body=%wide.region_4.10_spmd.clone.sunk | while | flops 4022007040 | bytes 30721944 | solution.py:105
  226.2 2.3 fusion.96
  228.6 2.2 fusion.97
  230.8 4.0 fusion.98
  243.1 2.3 fusion.96
  245.4 2.2 fusion.97
  247.7 4.0 fusion.98
  256.9 1.7 fusion.95
  259.9 2.3 fusion.96
  262.3 2.2 fusion.97
  264.5 4.0 fusion.98
  273.8 1.7 fusion.95
  276.8 2.3 fusion.96
  279.1 2.2 fusion.97
  281.4 4.0 fusion.98
  293.7 2.3 fusion.96
  296.0 2.2 fusion.97
  298.2 4.0 fusion.98
  310.5 2.3 fusion.96
  312.9 2.2 fusion.97
  315.1 4.0 fusion.98
  327.4 2.3 fusion.96
  329.7 2.2 fusion.97
  332.0 4.0 fusion.98
  344.2 2.3 fusion.96
  346.6 2.2 fusion.97
  348.8 4.0 fusion.98
  361.1 2.3 fusion.96
  363.4 2.2 fusion.97
  365.7 4.0 fusion.98
  377.9 2.3 fusion.96
  380.3 2.2 fusion.97
  382.5 4.0 fusion.98
  394.8 2.3 fusion.96
  397.1 2.2 fusion.97
  399.4 4.0 fusion.98
  411.7 2.3 fusion.96
  414.0 2.2 fusion.97
  416.3 4.0 fusion.98
  423.3 40.9 %all-reduce.2.cloned.1.call-done = f32[3,256,256]{2,1,0:T(8,128)} async-done(((f32[3,256,256]{2,1,0:T(8,128)}), f32[3,256,256]{2,1,0:T(8,128)}) %all-reduce.2.cloned.1.call-update) | async-done | bytes 786448 | tf_op jit(solution)/shard_map/psum | solution.py:106
  464.2 2.0 fusion.48
  (284 shorter events, 103.6 us)
Async XLA Ops:
  7.2 4.6 copy-start.6
  7.2 5.6 %copy-start.3 = (f32[32,2,2]{0,2,1:T(2,128)S(1)}, f32[32,2,2]{0,2,1:T(2,128)}, u32[]{:S(2)}) copy-start(f32[32,2,2]{0,2,1:T(2,128)} %param.14) | copy-start | bytes 1540
  7.2 6.5 %copy-start.4 = (f32[32,3]{0,1:T(4,128)S(1)}, f32[32,3]{0,1:T(4,128)}, u32[]{:S(2)}) copy-start(f32[32,3]{0,1:T(4,128)} %param.16) | copy-start | bytes 1156
  8.5 6.1 %copy-start.5 = (s32[32,3]{0,1:T(4,128)S(1)}, s32[32,3]{0,1:T(4,128)}, u32[]{:S(2)}) copy-start(s32[32,3]{0,1:T(4,128)} %param.15) | copy-start | bytes 1156
  10.4 14.5 %copy-start.1 = (f32[32,128,128]{2,1,0:T(8,128)S(1)}, f32[32,128,128]{2,1,0:T(8,128)}, u32[]{:S(2)}) copy-start(f32[32,128,128]{2,1,0:T(8,128)} %param.11) | copy-start | bytes 6291460
  16.5 35.1 %all-to-all-start = ((f32[32,3,11]{2,1,0:T(4,128)}), f32[32,3,11]{2,1,0:T(4,128)S(1)}, u32[]{:S(2)}, u32[]{:S(2)}) async-start(f32[32,3,11]{2,1,0:T(4,128)} %copy.90), calls=%async_computation | async-start | bytes 131072 | tf_op jit(solution)/shard_map/all_to_all | solution.py:90
  51.6 7.7 %copy-start.2 = (f32[8,2,41]{2,1,0:T(2,128)S(1)}, f32[8,2,41]{2,1,0:T(2,128)}, u32[]{:S(2)}) copy-start(f32[8,2,41]{2,1,0:T(2,128)} %param.17) | copy-start | bytes 7876
  51.6 168.5 %all-to-all-start.1 = ((f32[32,3,2,128,128]{4,3,2,1,0:T(8,128)}), f32[32,3,2,128,128]{4,3,2,1,0:T(8,128)}, u32[]{:S(2)}, u32[]{:S(2)}) async-start(f32[32,3,2,128,128]{4,3,2,1,0:T(8,128)} %broadcast_multiply_fusion), calls=%async_computation.1 | async-start | bytes 25165824 | tf_op jit(solution)/shard_map/all_to_all | solution.py:89
  59.3 404.9 %all-reduce.2.cloned.1.call-start = ((), (), s32[]{:S(2)}) async-start(), calls=%async_computation.2 | async-start | bytes 1572864 | tf_op jit(solution)/shard_map/psum | solution.py:106
  422.4 0.9 copy-start
Sparse Core Ops, SparseCore 0:
  423.5 40.6 all-reduce.1
where the time goes:
time: 474 us; the launch traced here: 473 us
  waiting for transfers between devices  202 us (43%)
  matrix products  153 us (32%)
  other arithmetic  47.6 us (10%)
  local copies, waits for them, and re-layouts  38.4 us (8%)
  starting transfers between devices  16.1 us (3%)
  between operations  14.3 us (3%)
    all_to_all x1, waiting for transfers between devices, shards(): lax.all_to_all(sent, 'patch', split_axis=0, concat_axis=0, tiled=True)  161 us
    dot_general x12, matrix products, warp_group(): both = jnp.einsum('gcpj,gqj->gcpq', left, cols_w, precision=HI)  47.7 us
    psum x1, waiting for transfers between devices, shards(): total = lax.psum(partial_value, 'visit')  40.9 us
    dot_general x12, matrix products, convolve(): return jnp.einsum('gbil,gbjl->gij', scaled, col_mats, precision=HI)  27.4 us
    dot_general x12, matrix products, warp_group(): left = jnp.einsum('gpi,gcij->gcpj', rows_w, planes, precision=HI)  26.9 us
    dot_general x12, matrix products, convolve(): partial_rows = jnp.einsum('gbik,gkl->gbil', row_mats, images, precision=HI)  20 us
    squeeze x24, local copies, waits for them, and re-layouts, shards(): partial_value = lax.scan(accumulate, start, (arrived, arrived_meta))[0]  15.7 us
    reduce_sum x12, other arithmetic, warp_group(): cover = jnp.sum(rows_w, 2)[:, :, None] * jnp.sum(cols_w, 2)[:, None, :]  15.5 us
  transfers between devices with their start and end apart: 3, of which 2 were waited for; matrix products, arithmetic and copies ran while one was open for 6% of the time, Pallas kernels for 0%

commit v1 on v0

--- a/solution.py
+++ b/solution.py
@@ -6,6 +6,15 @@
 PATCH = 256
 HI = lax.Precision.HIGHEST
 group_width = 8
+
+
+def prepare_teams_in(obj, axis_name):
+    chips = jax.lax.axis_size(axis_name)
+    found_now = lambda known: [(b, b ^ known) for b in range(chips)]
+    met_up = obj
+    for jj in range(chips.bit_length() - 1):
+        met_up = met_up + jax.lax.ppermute(met_up, axis_name, found_now(1 << jj))
+    return met_up
 
 
 def band_table(side, ntaps):
@@ -103,7 +112,7 @@
 
     start = jnp.zeros((3, PATCH, PATCH), jnp.float32)
     partial_value = lax.scan(accumulate, start, (arrived, arrived_meta))[0]
-    total = lax.psum(partial_value, "visit")
+    total = prepare_teams_in(partial_value, "visit")
     coadd, coadd_var = finish(total[0], total[1], total[2])
     return (coadd, coadd_var)
 

time: 474 us -> 452 us (0.954)
  waiting for transfers between devices: 202 us -> 187 us
  between operations: 14.3 us -> 0.93 us
  starting transfers between devices: 16.1 us -> 21.7 us
    psum x1 -> x0, waiting for transfers between devices: 40.9 us -> none  [shards(): total = lax.psum(partial_value, 'visit')]
    ppermute x0 -> x2, waiting for transfers between devices: none -> 26.3 us  [prepare_teams_in(): met_up = met_up + jax.lax.ppermute(met_up, axis_name, found_now(1 << jj))]
    ppermute x0 -> x2, starting transfers between devices: none -> 5.65 us  [prepare_teams_in(): met_up = met_up + jax.lax.ppermute(met_up, axis_name, found_now(1 << jj))]
  transfers between devices with their start and end apart: 3 -> 4, of which waited for: 2 -> 3; matrix products, arithmetic and copies ran while one was open for 6% -> 6% of each run, Pallas kernels for 0% -> 0%
where the time goes in v1:
time: 452 us; the launch traced here: 449 us
  waiting for transfers between devices  187 us (41%)
  matrix products  153 us (34%)
  other arithmetic  46.7 us (10%)
  local copies, waits for them, and re-layouts  37.5 us (8%)
  starting transfers between devices  21.7 us (5%)
    all_to_all x1, waiting for transfers between devices, shards(): lax.all_to_all(sent, 'patch', split_axis=0, concat_axis=0, tiled=True)  161 us
    dot_general x12, matrix products, warp_group(): both = jnp.einsum('gcpj,gqj->gcpq', left, cols_w, precision=HI)  47.7 us
    dot_general x12, matrix products, convolve(): return jnp.einsum('gbil,gbjl->gij', scaled, col_mats, precision=HI)  27.4 us
    dot_general x12, matrix products, warp_group(): left = jnp.einsum('gpi,gcij->gcpj', rows_w, planes, precision=HI)  26.9 us
    ppermute x2, waiting for transfers between devices, prepare_teams_in(): met_up = met_up + jax.lax.ppermute(met_up, axis_name, found_now(1 << jj))  26.3 us
    dot_general x12, matrix products, convolve(): partial_rows = jnp.einsum('gbik,gkl->gbil', row_mats, images, precision=HI)  20 us
    squeeze x24, local copies, waits for them, and re-layouts, shards(): partial_value = lax.scan(accumulate, start, (arrived, arrived_meta))[0]  15.7 us
    reduce_sum x12, other arithmetic, warp_group(): cover = jnp.sum(rows_w, 2)[:, :, None] * jnp.sum(cols_w, 2)[:, None, :]  15.5 us
  transfers between devices with their start and end apart: 4, of which 3 were waited for; matrix products, arithmetic and copies ran while one was open for 6% of the time, Pallas kernels for 0%

profile of v1, /device:TPU:0, one launch (start us, length us, event | category | flops | bytes accessed | tf_op | source)
XLA Modules:
  0.0 448.9 jit_solution(15638800382077173973)
XLA Ops:
  2.0 1.9 reduce_sum.75
  10.0 8.4 %all-to-all-start = ((f32[32,3,11]{2,1,0:T(4,128)}), f32[32,3,11]{2,1,0:T(4,128)S(1)}, u32[]{:S(2)}, u32[]{:S(2)}) async-start(f32[32,3,11]{2,1,0:T(4,128)} %copy.90), calls=%async_computation | async-start | bytes 131072 | tf_op jit(solution)/shard_map/all_to_all | solution.py:99
  18.4 3.9 pad_maximum_fusion.1
  22.3 10.9 %gather_fusion.5 = f32[96,2,128,128]{3,2,1,0:T(8,128)} fusion(f32[32,2,128,128]{3,2,0,1:T(8,128)} %pad_maximum_fusion.1, s32[1024]{0:T(1024)S(1)} %get-tuple-element.97), kind=kCustom, calls=%fused_computation.5 | custom fusion | bytes 25166208 | tf_op jit(solution)/shard_map/gather | solution.py:92
  33.3 11.8 %broadcast_multiply_fusion = f32[32,3,2,128,128]{4,3,2,1,0:T(8,128)} fusion(f32[32,3,2,128,128]{4,3,2,1,0:T(8,128)} %bitcast.135, f32[32,3]{1,0:T(8,128)S(1)} %reshape.285), kind=kLoop, calls=%fused_computation.74 | loop fusion | flops 3145728 | bytes 25166208 | tf_op jit(solution)/shard_map/mul | solution.py:92
  45.1 7.6 %all-to-all-start.1 = ((f32[32,3,2,128,128]{4,3,2,1,0:T(8,128)}), f32[32,3,2,128,128]{4,3,2,1,0:T(8,128)}, u32[]{:S(2)}, u32[]{:S(2)}) async-start(f32[32,3,2,128,128]{4,3,2,1,0:T(8,128)} %broadcast_multiply_fusion), calls=%async_computation.1 | async-start | bytes 25165824 | tf_op jit(solution)/shard_map/all_to_all | solution.py:98
  52.8 160.8 %all-to-all-done.1 = f32[32,3,2,128,128]{4,3,2,1,0:T(8,128)} async-done(((f32[32,3,2,128,128]{4,3,2,1,0:T(8,128)}), f32[32,3,2,128,128]{4,3,2,1,0:T(8,128)}, u32[]{:S(2)}, u32[]{:S(2)}) %all-to-all-start.1) | async-done | bytes 12582944 | tf_op jit(solution)/shard_map/all_to_all | solution.py:98
  213.6 202.3 %while.11 = (s32[]{:T(128)}, f32[3,256,256]{2,1,0:T(8,128)S(1)}, f32[12,8,11]{2,1,0:T(8,128)S(1)}, f32[8,2,41]{2,0,1:T(8,128)S(1)}, f32[12,8,2,128,128]{4,3,2,1,0:T(8,128)}, /*index=5*/s32[]{:T(128)}, s32[]{:T(128)}) while((s32[]{:T(128)}, f32[3,256,256]{2,1,0:T(8,128)S(1)}, f32[12,8,11]{2,1,0:T(8,128)S(1)}, ...), condition=%wide.region_10.11_spmd.clone, body=%wide.region_4.10_spmd.clone.sunk | while | flops 4022007040 | bytes 30721944 | solution.py:114
  219.7 2.3 fusion.96
  222.0 2.2 fusion.97
  224.3 4.0 fusion.98
  236.5 2.3 fusion.96
  238.9 2.2 fusion.97
  241.1 4.0 fusion.98
  250.4 1.7 fusion.95
  253.4 2.3 fusion.96
  255.7 2.2 fusion.97
  258.0 4.0 fusion.98
  270.3 2.3 fusion.96
  272.6 2.2 fusion.97
  274.8 4.0 fusion.98
  287.1 2.3 fusion.96
  289.5 2.2 fusion.97
  291.7 4.0 fusion.98
  304.0 2.3 fusion.96
  306.3 2.2 fusion.97
  308.6 4.0 fusion.98
  320.8 2.3 fusion.96
  323.2 2.2 fusion.97
  325.4 4.0 fusion.98
  337.7 2.3 fusion.96
  340.0 2.2 fusion.97
  342.3 4.0 fusion.98
  354.6 2.3 fusion.96
  356.9 2.2 fusion.97
  359.1 4.0 fusion.98
  371.4 2.3 fusion.96
  373.8 2.2 fusion.97
  376.0 4.0 fusion.98
  388.3 2.3 fusion.96
  390.6 2.2 fusion.97
  392.9 4.0 fusion.98
  405.1 2.3 fusion.96
  407.5 2.2 fusion.97
  409.7 4.0 fusion.98
  417.4 16.3 %collective-permute-done = f32[3,256,256]{2,1,0:T(8,128)S(1)} collective-permute-done((f32[3,256,256]{2,1,0:T(8,128)S(1)}, f32[3,256,256]{2,1,0:T(8,128)S(1)}, u32[]{:S(2)}, u32[]{:S(2)}) %collective-permute-start) | collective-permute-done | bytes 786464 | tf_op jit(solution)/shard_map/ppermute | solution.py:16
  433.9 4.1 collective-permute-start.1
  438.0 10.0 %collective-permute-done.1 = f32[3,256,256]{2,1,0:T(8,128)S(1)} collective-permute-done((f32[3,256,256]{2,1,0:T(8,128)S(1)}, f32[3,256,256]{2,1,0:T(8,128)S(1)}, u32[]{:S(2)}, u32[]{:S(2)}) %collective-permute-start.1) | collective-permute-done | bytes 786464 | tf_op jit(solution)/shard_map/ppermute | solution.py:16
  (285 shorter events, 106.9 us)
Async XLA Ops:
  0.6 4.6 %copy-start.5 = (s32[32,2,2]{0,2,1:T(2,128)S(1)}, s32[32,2,2]{0,2,1:T(2,128)}, u32[]{:S(2)}) copy-start(s32[32,2,2]{0,2,1:T(2,128)} %param.13) | copy-start | bytes 1540
  0.6 5.6 %copy-start.2 = (f32[32,2,2]{0,2,1:T(2,128)S(1)}, f32[32,2,2]{0,2,1:T(2,128)}, u32[]{:S(2)}) copy-start(f32[32,2,2]{0,2,1:T(2,128)} %param.14) | copy-start | bytes 1540
  0.7 6.5 %copy-start.3 = (f32[32,3]{0,1:T(4,128)S(1)}, f32[32,3]{0,1:T(4,128)}, u32[]{:S(2)}) copy-start(f32[32,3]{0,1:T(4,128)} %param.16) | copy-start | bytes 1156
  1.9 6.1 %copy-start.4 = (s32[32,3]{0,1:T(4,128)S(1)}, s32[32,3]{0,1:T(4,128)}, u32[]{:S(2)}) copy-start(s32[32,3]{0,1:T(4,128)} %param.15) | copy-start | bytes 1156
  3.9 14.5 %copy-start = (f32[32,128,128]{2,1,0:T(8,128)S(1)}, f32[32,128,128]{2,1,0:T(8,128)}, u32[]{:S(2)}) copy-start(f32[32,128,128]{2,1,0:T(8,128)} %param.11) | copy-start | bytes 6291460
  10.0 35.1 %all-to-all-start = ((f32[32,3,11]{2,1,0:T(4,128)}), f32[32,3,11]{2,1,0:T(4,128)S(1)}, u32[]{:S(2)}, u32[]{:S(2)}) async-start(f32[32,3,11]{2,1,0:T(4,128)} %copy.90), calls=%async_computation | async-start | bytes 131072 | tf_op jit(solution)/shard_map/all_to_all | solution.py:99
  45.1 7.6 %copy-start.1 = (f32[8,2,41]{2,1,0:T(2,128)S(1)}, f32[8,2,41]{2,1,0:T(2,128)}, u32[]{:S(2)}) copy-start(f32[8,2,41]{2,1,0:T(2,128)} %param.17) | copy-start | bytes 7876
  45.1 168.5 %all-to-all-start.1 = ((f32[32,3,2,128,128]{4,3,2,1,0:T(8,128)}), f32[32,3,2,128,128]{4,3,2,1,0:T(8,128)}, u32[]{:S(2)}, u32[]{:S(2)}) async-start(f32[32,3,2,128,128]{4,3,2,1,0:T(8,128)} %broadcast_multiply_fusion), calls=%async_computation.1 | async-start | bytes 25165824 | tf_op jit(solution)/shard_map/all_to_all | solution.py:98
  415.9 17.9 %collective-permute-start = (f32[3,256,256]{2,1,0:T(8,128)S(1)}, f32[3,256,256]{2,1,0:T(8,128)S(1)}, u32[]{:S(2)}, u32[]{:S(2)}) collective-permute-start(f32[3,256,256]{2,1,0:T(8,128)S(1)} %get-tuple-element.29), channel_id=1, source_target_pairs={{0,32},{32,0},{64,96},{96,64},{1,33},{33,1},{65,97},{97,65},{2,34}... | collective-permute-start | bytes 2359304 | tf_op jit(solution)/shard_map/ppermute | solution.py:16
  433.9 14.1 %collective-permute-start.1 = (f32[3,256,256]{2,1,0:T(8,128)S(1)}, f32[3,256,256]{2,1,0:T(8,128)S(1)}, u32[]{:S(2)}, u32[]{:S(2)}) collective-permute-start(f32[3,256,256]{2,1,0:T(8,128)S(1)} %add.63), channel_id=1, source_target_pairs={{0,64},{32,96},{64,0},{96,32},{1,65},{33,97},{65,1},{97,33},{2,66}... | collective-permute-start | bytes 2359304 | tf_op jit(solution)/shard_map/ppermute | solution.py:16
